TPU v7x, 32 devices: a whole 2x2x4 slice. The times are simulated.
32 devices in a mesh: shard: 16 (over z, x, core), ctx: 2 (over y).
Axes of the slice: x: 2, y: 2, z: 4, core: 2. Of those that a mesh axis runs over, the one named last changes fastest.
Arguments:
- tokens: bfloat16 [8192, 576], P(('shard', 'ctx')), may hold values from -6 to 6
- cotangent: bfloat16 [8192, 576], P(('shard', 'ctx')), may hold values from -6 to 6
- seq_lengths: int32 [16], P('shard'), may hold values from 64 to 512, as said below
- attn_params: float32 [885888], P('shard')
- attn_first: float32 [885888], P('shard'), may hold values from -6 to 6
- attn_second: float32 [885888], P('shard'), may hold values from 1 to 100
- ffn_params: float32 [2654208], P('shard')
- ffn_first: float32 [2654208], P('shard'), may hold values from -6 to 6
- ffn_second: float32 [2654208], P('shard'), may hold values from 1 to 100
Outputs:
- outputs: bfloat16 [8192, 576], P(('shard', 'ctx'))
- grad_tokens: bfloat16 [8192, 576], P(('shard', 'ctx'))
- attn_grad: float32 [885888], P('shard')
- ffn_grad: float32 [2654208], P('shard')
- attn_new: float32 [885888], P('shard')
- attn_first_new: float32 [885888], P('shard')
- attn_second_new: float32 [885888], P('shard')
- ffn_new: float32 [2654208], P('shard')
- ffn_first_new: float32 [2654208], P('shard')
- ffn_second_new: float32 [2654208], P('shard')
Inputs may be any that keep to these rules, and one draw needn't show every extreme that they name: `seq_lengths`: in every draw some sequence fills all 512 slots.
All inputs are finite; a program needn't handle non-finite values.
Results may differ from a plain program's by a relative error of at most 0.01.
The roundings to bfloat16 on the way count: a program that leaves them out, or rounds other values in their place, can miss the bound.
Values may be sent and summed in bfloat16 or wider, within the bound.
A program may use at most 128 MiB of HBM per device.

v0:
```python
import math
import jax
import jax.numpy as jnp
from jax import lax
from jax.sharding import PartitionSpec as P

MODEL_WIDTH = 576
QUERY_HEADS = 9
KEY_VALUE_HEADS = 3
HEAD_SIZE = 64
FF = 1536
ADAM_STEP = 3
rms_eps = 1e-05
rope_base = 100000.0
beta_one = 0.9
beta_two = 0.95
learn_rate = 0.02
decay_rate = 0.1
adam_eps = 1e-08
masked_score = -1e30


def split_flattened(flattened, shapes):
    pieces = []
    offset = 0
    for shape in shapes:
        width = 1
        for extent in shape:
            width = width * extent
        pieces.append(flattened[offset : offset + width].reshape(shape))
        offset = offset + width
    return pieces


def split_attention(flattened):
    return split_flattened(
        flattened,
        (
            (MODEL_WIDTH, QUERY_HEADS * HEAD_SIZE),
            (MODEL_WIDTH, KEY_VALUE_HEADS * HEAD_SIZE),
            (MODEL_WIDTH, KEY_VALUE_HEADS * HEAD_SIZE),
            (QUERY_HEADS * HEAD_SIZE, MODEL_WIDTH),
            (MODEL_WIDTH,),
            (MODEL_WIDTH,),
        ),
    )


def split_feedforward(flattened):
    return split_flattened(flattened, ((MODEL_WIDTH, FF), (MODEL_WIDTH, FF), (FF, MODEL_WIDTH)))


def rope_tables(positions):
    index = jnp.arange(HEAD_SIZE // 2).astype(jnp.float32)
    inverse = jnp.exp(index * (-2.0 * math.log(rope_base) / HEAD_SIZE))
    angles = positions.astype(jnp.float32)[:, None] * inverse[None, :]
    angles = jnp.concatenate([angles, angles], axis=1)
    return (jnp.cos(angles), jnp.sin(angles))


def apply_rotation(values, cosine_table, sine_table):
    half = values.shape[-1] // 2
    turned = jnp.concatenate([-values[..., half:], values[..., :half]], axis=-1)
    return values * cosine_table[:, None, :] + turned * sine_table[:, None, :]


def reverse_rotation(grads, cosine_table, sine_table):
    half = grads.shape[-1] // 2
    weighted = grads * sine_table[:, None, :]
    turned = jnp.concatenate([weighted[..., half:], -weighted[..., :half]], axis=-1)
    return grads * cosine_table[:, None, :] + turned


def norm_rows(values, gain):
    mean_sq = jnp.mean(values * values, axis=-1, keepdims=True)
    inverse = lax.rsqrt(mean_sq + rms_eps)
    scaled = values * inverse
    return (scaled, inverse, (scaled * gain).astype(jnp.bfloat16))


def norm_back(grad_normed, scaled, inverse, gain):
    grad_scaled = grad_normed * gain
    grad_gain = jnp.sum(grad_normed * scaled, axis=0)
    inner = jnp.mean(grad_scaled * scaled, axis=-1, keepdims=True)
    return (inverse * (grad_scaled - scaled * inner), grad_gain)


def attend(query_rows, keys, values, mask):
    row_entries = query_rows.shape[0]
    scale = 1.0 / math.sqrt(HEAD_SIZE)
    grouped_heads = query_rows.reshape(
        row_entries, KEY_VALUE_HEADS, QUERY_HEADS // KEY_VALUE_HEADS, HEAD_SIZE
    )
    scores = (
        jnp.einsum("tkgd,skd->kgts", grouped_heads, keys, preferred_element_type=jnp.float32)
        * scale
    )
    scores = jnp.where(mask[None, None], scores, masked_score)
    top = jnp.max(scores, axis=-1, keepdims=True)
    total = jnp.sum(jnp.exp(scores - top), axis=-1, keepdims=True)
    log_total = top + jnp.log(total)
    probs = jnp.exp(scores - log_total).astype(jnp.bfloat16)
    mixture = jnp.einsum("kgts,skd->tkgd", probs, values, preferred_element_type=jnp.float32)
    return (mixture.reshape(row_entries, QUERY_HEADS * HEAD_SIZE).astype(jnp.bfloat16), log_total)


def attend_back(query_rows, keys, values, mask, log_total, mixture, mixture_gradient):
    row_entries = query_rows.shape[0]
    head_group = QUERY_HEADS // KEY_VALUE_HEADS
    scale = 1.0 / math.sqrt(HEAD_SIZE)
    grouped_queries = query_rows.reshape(
        row_entries, KEY_VALUE_HEADS, head_group, HEAD_SIZE
    ).transpose(1, 0, 2, 3)
    gradient_groups = mixture_gradient.reshape(
        row_entries, KEY_VALUE_HEADS, head_group, HEAD_SIZE
    ).transpose(1, 0, 2, 3)
    mixture_groups = mixture.reshape(row_entries, KEY_VALUE_HEADS, head_group, HEAD_SIZE).transpose(
        1, 0, 2, 3
    )
    key_groups = keys.transpose(1, 0, 2)
    value_groups = values.transpose(1, 0, 2)

    def one_group(item):
        query_one, key_one, value_one, total_one, mixed_one, grad_one = item
        scores = (
            jnp.einsum("tgd,sd->gts", query_one, key_one, preferred_element_type=jnp.float32)
            * scale
        )
        scores = jnp.where(mask[None], scores, masked_score)
        probs = jnp.exp(scores - total_one)
        delta = jnp.einsum("tgd,tgd->gt", grad_one, mixed_one, preferred_element_type=jnp.float32)
        grad_probs = jnp.einsum(
            "tgd,sd->gts", grad_one, value_one, preferred_element_type=jnp.float32
        )
        grad_scores = (probs * (grad_probs - delta[..., None]) * scale).astype(jnp.bfloat16)
        grad_query = jnp.einsum(
            "gts,sd->tgd", grad_scores, key_one, preferred_element_type=jnp.float32
        )
        key_gradient = jnp.einsum(
            "gts,tgd->sd", grad_scores, query_one, preferred_element_type=jnp.float32
        )
        value_gradient = jnp.einsum(
            "gts,tgd->sd", probs.astype(jnp.bfloat16), grad_one, preferred_element_type=jnp.float32
        )
        return (grad_query, key_gradient, value_gradient)

    grad_query, key_gradient, value_gradient = lax.map(
        one_group,
        (grouped_queries, key_groups, value_groups, log_total, mixture_groups, gradient_groups),
    )
    grad_query = grad_query.transpose(1, 0, 2, 3).reshape(row_entries, QUERY_HEADS, HEAD_SIZE)
    return (grad_query, key_gradient.transpose(1, 0, 2), value_gradient.transpose(1, 0, 2))


def adam_update(params, first, second, grads):
    first_new = beta_one * first + (1.0 - beta_one) * grads
    second_new = beta_two * second + (1.0 - beta_two) * grads * grads
    corr_one = 1.0 - beta_one**ADAM_STEP
    corr_two = 1.0 - beta_two**ADAM_STEP
    moved = first_new / corr_one / (jnp.sqrt(second_new / corr_two) + adam_eps)
    return (params - learn_rate * (moved + decay_rate * params), first_new, second_new)


def owner_layout(term, owners, pair):
    columns = term.shape[0] // owners
    padded_columns = columns + -columns % pair
    table = term.reshape(owners, columns)
    return (jnp.pad(table, ((0, 0), (0, padded_columns - columns))).reshape(-1), columns)


def body(
    tokens,
    cotangent,
    seq_lengths,
    attn_params,
    attn_first,
    attn_second,
    ffn_params,
    ffn_first,
    ffn_second,
):
    row_entries = tokens.shape[0]
    ctx_count = lax.axis_size("ctx")
    ctx_index = lax.axis_index("ctx")
    owners = lax.axis_size("shard")
    slot_entries = row_entries * ctx_count
    length = seq_lengths[0]
    low_params = (attn_params.astype(jnp.bfloat16), ffn_params.astype(jnp.bfloat16))
    attn_whole, ffn_whole = (
        lax.all_gather(low_params[0], "shard", axis=0, tiled=True),
        lax.all_gather(low_params[1], "shard", axis=0, tiled=True),
    )
    w_query, key_matrix, value_matrix, w_out, gain_one, gain_two = split_attention(attn_whole)
    w_gate, w_up, w_down = split_feedforward(ffn_whole)
    gain_one = gain_one.astype(jnp.float32)
    gain_two = gain_two.astype(jnp.float32)
    positions = ctx_index * row_entries + jnp.arange(row_entries)
    key_positions = jnp.arange(slot_entries)
    valid = (positions < length).astype(jnp.float32)[:, None]
    has_rows = ctx_index * row_entries < length
    mask = (key_positions[None, :] <= positions[:, None]) & (key_positions[None, :] < length)
    inputs = tokens.astype(jnp.float32)
    scaled_one, inv_one, first_normed = norm_rows(inputs, gain_one)
    query_raw = jnp.dot(first_normed, w_query, preferred_element_type=jnp.float32).reshape(
        row_entries, QUERY_HEADS, HEAD_SIZE
    )
    unrotated_key = jnp.dot(first_normed, key_matrix, preferred_element_type=jnp.float32).reshape(
        row_entries, KEY_VALUE_HEADS, HEAD_SIZE
    )
    value_reduced = jnp.dot(first_normed, value_matrix, preferred_element_type=jnp.float32).astype(
        jnp.bfloat16
    )
    cosine_table, sine_table = rope_tables(positions)
    query_low = apply_rotation(query_raw, cosine_table, sine_table).astype(jnp.bfloat16)
    key_reduced = (
        apply_rotation(unrotated_key, cosine_table, sine_table)
        .astype(jnp.bfloat16)
        .reshape(row_entries, KEY_VALUE_HEADS * HEAD_SIZE)
    )
    full_keys, full_values = (
        lax.all_gather(key_reduced, "ctx", axis=0, tiled=True),
        lax.all_gather(value_reduced, "ctx", axis=0, tiled=True),
    )
    full_keys = full_keys.reshape(slot_entries, KEY_VALUE_HEADS, HEAD_SIZE)
    full_values = full_values.reshape(slot_entries, KEY_VALUE_HEADS, HEAD_SIZE)
    mixture, log_total = lax.cond(
        has_rows,
        lambda: attend(query_low, full_keys, full_values, mask),
        lambda: (
            jnp.zeros((row_entries, QUERY_HEADS * HEAD_SIZE), jnp.bfloat16),
            jnp.zeros(
                (KEY_VALUE_HEADS, QUERY_HEADS // KEY_VALUE_HEADS, row_entries, 1), jnp.float32
            ),
        ),
    )
    hidden = inputs + jnp.dot(mixture, w_out, preferred_element_type=jnp.float32)
    scaled_two, inv_two, normed_two = norm_rows(hidden, gain_two)
    gate = jnp.dot(normed_two, w_gate, preferred_element_type=jnp.float32)
    upward = jnp.dot(normed_two, w_up, preferred_element_type=jnp.float32)
    sigma = jax.nn.sigmoid(gate)
    activ = (gate * sigma * upward).astype(jnp.bfloat16)
    result = hidden + jnp.dot(activ, w_down, preferred_element_type=jnp.float32)
    outputs = (valid * result).astype(jnp.bfloat16)
    grad_result = valid * cotangent.astype(jnp.float32)
    grad_low = grad_result.astype(jnp.bfloat16)
    grad_w_down = jnp.dot(activ.T, grad_low, preferred_element_type=jnp.float32)
    grad_activ = jnp.dot(grad_low, w_down.T, preferred_element_type=jnp.float32)
    grad_gate = (grad_activ * upward * sigma * (1.0 + gate * (1.0 - sigma))).astype(jnp.bfloat16)
    grad_upward = (grad_activ * gate * sigma).astype(jnp.bfloat16)
    grad_w_gate = jnp.dot(normed_two.T, grad_gate, preferred_element_type=jnp.float32)
    grad_w_up = jnp.dot(normed_two.T, grad_upward, preferred_element_type=jnp.float32)
    ffn_term = jnp.concatenate(
        [grad_w_gate.reshape(-1), grad_w_up.reshape(-1), grad_w_down.reshape(-1)]
    )
    ffn_padded, ffn_columns = owner_layout(ffn_term, owners, ctx_count)
    grad_normed_two = jnp.dot(grad_gate, w_gate.T, preferred_element_type=jnp.float32) + jnp.dot(
        grad_upward, w_up.T, preferred_element_type=jnp.float32
    )
    grad_hidden_part, grad_gain_two = norm_back(grad_normed_two, scaled_two, inv_two, gain_two)
    grad_hidden = grad_result + grad_hidden_part
    grad_hidden_low = grad_hidden.astype(jnp.bfloat16)
    grad_w_out = jnp.dot(mixture.T, grad_hidden_low, preferred_element_type=jnp.float32)
    mixture_gradient = jnp.dot(grad_hidden_low, w_out.T, preferred_element_type=jnp.float32).astype(
        jnp.bfloat16
    )
    grad_query, full_key_gradient, full_value_gradient = lax.cond(
        has_rows,
        lambda: attend_back(
            query_low, full_keys, full_values, mask, log_total, mixture, mixture_gradient
        ),
        lambda: (
            jnp.zeros((row_entries, QUERY_HEADS, HEAD_SIZE), jnp.float32),
            jnp.zeros((slot_entries, KEY_VALUE_HEADS, HEAD_SIZE), jnp.float32),
            jnp.zeros((slot_entries, KEY_VALUE_HEADS, HEAD_SIZE), jnp.float32),
        ),
    )
    key_gradient, value_gradient = (
        lax.psum_scatter(
            full_key_gradient.reshape(slot_entries, KEY_VALUE_HEADS * HEAD_SIZE),
            "ctx",
            scatter_dimension=0,
            tiled=True,
        ),
        lax.psum_scatter(
            full_value_gradient.reshape(slot_entries, KEY_VALUE_HEADS * HEAD_SIZE),
            "ctx",
            scatter_dimension=0,
            tiled=True,
        ),
    )
    grad_query_raw = (
        reverse_rotation(grad_query, cosine_table, sine_table)
        .astype(jnp.bfloat16)
        .reshape(row_entries, QUERY_HEADS * HEAD_SIZE)
    )
    unrotated_key_gradient = (
        reverse_rotation(
            key_gradient.reshape(row_entries, KEY_VALUE_HEADS, HEAD_SIZE), cosine_table, sine_table
        )
        .astype(jnp.bfloat16)
        .reshape(row_entries, KEY_VALUE_HEADS * HEAD_SIZE)
    )
    plain_value_gradient = value_gradient.astype(jnp.bfloat16)
    grad_w_query = jnp.dot(first_normed.T, grad_query_raw, preferred_element_type=jnp.float32)
    grad_w_key = jnp.dot(first_normed.T, unrotated_key_gradient, preferred_element_type=jnp.float32)
    grad_w_value = jnp.dot(first_normed.T, plain_value_gradient, preferred_element_type=jnp.float32)
    grad_normed_one = jnp.dot(grad_query_raw, w_query.T, preferred_element_type=jnp.float32)
    grad_normed_one = grad_normed_one + jnp.dot(
        unrotated_key_gradient, key_matrix.T, preferred_element_type=jnp.float32
    )
    grad_normed_one = grad_normed_one + jnp.dot(
        plain_value_gradient, value_matrix.T, preferred_element_type=jnp.float32
    )
    grad_input_part, grad_gain_one = norm_back(grad_normed_one, scaled_one, inv_one, gain_one)
    grad_tokens = (grad_hidden + grad_input_part).astype(jnp.bfloat16)
    attn_term = jnp.concatenate(
        [
            grad_w_query.reshape(-1),
            grad_w_key.reshape(-1),
            grad_w_value.reshape(-1),
            grad_w_out.reshape(-1),
            grad_gain_one,
            grad_gain_two,
        ]
    )
    attn_padded, attn_columns = owner_layout(attn_term, owners, ctx_count)
    attn_half, ffn_half = (
        lax.psum_scatter(attn_padded, ("shard", "ctx"), scatter_dimension=0, tiled=True),
        lax.psum_scatter(ffn_padded, ("shard", "ctx"), scatter_dimension=0, tiled=True),
    )
    attn_joined, ffn_joined = (
        lax.all_gather(attn_half, "ctx", axis=0, tiled=True),
        lax.all_gather(ffn_half, "ctx", axis=0, tiled=True),
    )
    attn_grad = attn_joined[:attn_columns]
    attn_new, attn_first_new, attn_second_new = adam_update(
        attn_params, attn_first, attn_second, attn_grad
    )
    ffn_new, ffn_first_new, ffn_second_new = adam_update(
        ffn_params, ffn_first, ffn_second, ffn_joined
    )
    return (
        outputs,
        grad_tokens,
        attn_grad,
        ffn_joined,
        attn_new,
        attn_first_new,
        attn_second_new,
        ffn_new,
        ffn_first_new,
        ffn_second_new,
    )


def solution(mesh):
    return jax.shard_map(
        body,
        mesh=mesh,
        in_specs=(
            P(("shard", "ctx"), None),
            P(("shard", "ctx"), None),
            P("shard"),
            P("shard"),
            P("shard"),
            P("shard"),
            P("shard"),
            P("shard"),
            P("shard"),
        ),
        out_specs=(
            P(("shard", "ctx"), None),
            P(("shard", "ctx"), None),
            P("shard"),
            P("shard"),
            P("shard"),
            P("shard"),
            P("shard"),
            P("shard"),
            P("shard"),
            P("shard"),
        ),
        check_vma=False,
    )
```

profile of v0, /device:TPU:0, one launch (start us, length us, event | category | flops | bytes accessed | tf_op | source)
XLA Modules:
  0.0 597.9 jit_solution(964759938562371816)
XLA Ops:
  16.1 95.9 %all-reduce.9.cloned.1.call-done = bf16[885888]{0:T(1024)(128)(2,1)} async-done(((bf16[885888]{0:T(1024)(128)(2,1)}), bf16[885888]{0:T(1024)(128)(2,1)}) %all-reduce.9.cloned.1.call-update) | async-done | bytes 1771792
  119.5 5.3 all_gather.19
  125.2 5.3 all_gather.20
  131.9 4.6 conditional.2
  137.3 33.6 %all-gather.2.cloned.1.call-done = bf16[2654208]{0:T(1024)(128)(2,1)} async-done(((bf16[165888]{0:T(1024)(128)(2,1)}), bf16[2654208]{0:T(1024)(128)(2,1)}) %all-gather.2.cloned.1.call-update) | async-done | bytes 5308432 | tf_op jit(solution)/shard_map/all_gather | solution.py:191
  170.9 4.7 fusion.88
  175.6 3.0 slice.124
  178.6 3.6 slice.126
  182.1 3.4 fusion.93
  187.5 4.3 slice.128
  191.9 4.8 multiply_convert_fusion
  201.8 27.9 %conditional.3 = (f32[256,9,64]{0,2,1:T(8,128)}, f32[512,3,64]{0,2,1:T(8,128)}, f32[512,3,64]{0,2,1:T(8,128)}) conditional(s32[]{:T(128)} %convert_element_type.112, () %tuple.30, (bf16[256,9,64]{0,2,1:T(8,128)(2,1)S(1)}, bf16[512,3,64]{0,2,1:T(8,128)(2,1)}, bf16[512,3,64]{0,2,1:T(8,128)(2,1)}, bf16[256,576]{0,1:T(8,128)(2,1)S(1)}, ...), branch_computations={%region_7.8_spmd, %region_8.0_spmd} | conditional | flops 254999808 | bytes 16739761 | solution.py:266
  201.8 27.9 %while.13 = (s32[]{:T(128)}, f32[3,256,3,64]{1,3,2,0:T(8,128)}, f32[3,512,64]{1,2,0:T(8,128)}, f32[3,512,64]{1,2,0:T(8,128)}, bf16[3,512,64]{1,2,0:T(8,128)(2,1)...) while((s32[]{:T(128)}, f32[3,256,3,64]{1,3,2,0:T(8,128)}, ...), condition=%wide.region_10.10_spmd, body=%wide.region_9.9_spmd.sunk | while | flops 254999808 | bytes 16739633 | solution.py:147
  231.2 2.7 fusion.61
  239.9 5.4 reshape.299
  247.6 4.6 reshape.298
  254.7 4.6 reshape.297
  259.3 11.2 %pad_maximum_fusion = f32[2654208]{0:T(1024)} fusion(f32[884736]{0:T(1024)} %reshape.299, f32[884736]{0:T(1024)} %reshape.298, f32[884736]{0:T(1024)} %reshape.297), kind=kLoop, calls=%fused_computation.50 | loop fusion | flops 5308416 | bytes 21233664 | tf_op jit(solution)/shard_map/concatenate | solution.py:252
  283.2 2.9 fusion.50
  286.1 25.4 %concatenate.37 = f32[885888]{0:T(1024)} concatenate(f32[331776]{0:T(1024)S(1)} %copy-done.16, f32[110592]{0:T(1024)} %reshape.294, f32[110592]{0:T(1024)} %reshape.295, f32[331776]{0:T(1024)S(1)} %reshape.296, f32[576]{0:T(1024)S(1)} %get-tuple-element.157, f32[576]{0:T(1024)S(1)} %copy-done.48), dimensions={0} | concatenate | bytes 7087104 | tf_op jit(solution)/shard_map/concatenate | solution.py:316
  313.4 2.8 fusion.38
  317.2 242.8 %all-reduce.13.cloned.1.call-done = (f32[885888]{0:T(1024)}, f32[2654208]{0:T(1024)}) async-done(((f32[885888]{0:T(1024)}, f32[2654208]{0:T(1024)}), (f32[885888]{0:T(1024)}, f32[2654208]{0:T(1024)})) %all-reduce.13.cloned.1.call-update) | async-done | bytes 14160400
  563.3 12.8 %all_gather.23 = f32[165888]{0:T(1024)S(1)} all-gather(f32[82944]{0:T(1024)S(1)} %dynamic-slice.3), channel_id=1, replica_groups=mesh['shard'=16,'ctx'=2] {'ctx'}, dimensions={0}, use_global_device_ids=true | all-gather | bytes 995328 | tf_op jit(solution)/shard_map/all_gather | solution.py:333
  577.7 8.9 %all-reduce.11.cloned.1.call-done = f32[55368]{0:T(1024)} async-done(((f32[55368]{0:T(1024)}), f32[55368]{0:T(1024)}) %all-reduce.11.cloned.1.call-update) | async-done | bytes 221488
  (258 shorter events, 92.6 us)
Async XLA Ops:
  7.2 104.9 %all-reduce.9.cloned.1.call-start = ((), (), s32[]{:S(2)}) async-start(), calls=%async_computation.5 | async-start | bytes 3547136
  12.7 158.1 %all-gather.2.cloned.1.call-start = ((), (), s32[]{:S(2)}) async-start(), calls=%async_computation.2 | async-start | bytes 5640192 | tf_op jit(solution)/shard_map/all_gather | solution.py:191
  13.6 257.0 %reduce-scatter.3.cloned.1.call-start = ((), (), s32[]{:S(2)}) async-start(), calls=%async_computation.3 | async-start | bytes 589824 | tf_op jit(solution)/shard_map/reduce_scatter | solution.py:278
  14.7 116.4 %copy-start.32 = (f32[256,64]{0,1:T(8,128)}, f32[256,64]{0,1:T(8,128)S(1)}, u32[]{:S(2)}) copy-start(f32[256,64]{0,1:T(8,128)S(1)} %get-tuple-element.211) | copy-start | bytes 196612
  14.7 116.4 %copy-start.34 = (f32[256,64]{0,1:T(8,128)}, f32[256,64]{0,1:T(8,128)S(1)}, u32[]{:S(2)}) copy-start(f32[256,64]{0,1:T(8,128)S(1)} %get-tuple-element.212) | copy-start | bytes 196612
  116.7 8.1 %copy-start.38 = (bf16[576,192]{1,0:T(8,128)(2,1)}, bf16[576,192]{1,0:T(8,128)(2,1)S(1)}, u32[]{:S(2)}) copy-start(bf16[576,192]{1,0:T(8,128)(2,1)S(1)} %reshape.286) | copy-start | bytes 663556
  117.3 19.3 %copy-start.10 = (bf16[576,576]{1,0:T(8,128)(2,1)}, bf16[576,576]{1,0:T(8,128)(2,1)S(1)}, u32[]{:S(2)}) copy-start(bf16[576,576]{1,0:T(8,128)(2,1)S(1)} %reshape.288) | copy-start | bytes 1990660
  124.8 7.1 %copy-start.30 = (bf16[512,192]{0,1:T(8,128)(2,1)}, bf16[512,192]{0,1:T(8,128)(2,1)S(1)}, u32[]{:S(2)}) copy-start(bf16[512,192]{0,1:T(8,128)(2,1)S(1)} %all_gather.19) | copy-start | bytes 589828
  137.2 48.3 %copy-start.7 = (bf16[256,576]{0,1:T(8,128)(2,1)}, bf16[256,576]{0,1:T(8,128)(2,1)S(1)}, u32[]{:S(2)}) copy-start(bf16[256,576]{0,1:T(8,128)(2,1)S(1)} %multiply_convert_fusion.3) | copy-start | bytes 884740
  229.7 49.2 %reduce-scatter.5.cloned.1.call-start = ((), (), s32[]{:S(2)}) async-start(), calls=%async_computation.4 | async-start | bytes 589824 | tf_op jit(solution)/shard_map/reduce_scatter | solution.py:284
  239.9 5.4 copy-start.8
  239.9 5.4 copy-start.20
  259.3 11.3 %copy-start.35 = (f32[256,64]{0,1:T(8,128)S(1)}, f32[256,64]{0,1:T(8,128)}, u32[]{:S(2)}) copy-start(f32[256,64]{0,1:T(8,128)} %copy-done.34) | copy-start | bytes 196612
  259.3 300.8 %all-reduce.13.cloned.1.call-start = ((), (), s32[]{:S(2)}) async-start(), calls=%async_computation.7 | async-start | bytes 28327936
  271.6 6.1 %copy-start.13 = (bf16[576,576]{1,0:T(8,128)(2,1)S(1)}, bf16[576,576]{1,0:T(8,128)(2,1)}, u32[]{:S(2)}) copy-start(bf16[576,576]{1,0:T(8,128)(2,1)} %copy-done.12) | copy-start | bytes 1990660
  271.6 6.1 %copy-start.25 = (bf16[256,9,64]{0,2,1:T(8,128)(2,1)S(1)}, bf16[256,9,64]{0,2,1:T(8,128)(2,1)}, u32[]{:S(2)}) copy-start(bf16[256,9,64]{0,2,1:T(8,128)(2,1)} %copy-done.24) | copy-start | bytes 884740
  280.9 5.2 copy-start.48
  311.5 275.1 %all-reduce.11.cloned.1.call-start = ((), (), s32[]{:S(2)}) async-start(), calls=%async_computation.6 | async-start | bytes 450560
  316.3 259.8 %copy-start.27 = (f32[165888]{0:T(1024)S(1)}, f32[165888]{0:T(1024)}, u32[]{:S(2)}) copy-start(f32[165888]{0:T(1024)} %param.21) | copy-start | bytes 1990660
  316.3 259.8 %copy-start.44 = (f32[165888]{0:T(1024)S(1)}, f32[165888]{0:T(1024)}, u32[]{:S(2)}) copy-start(f32[165888]{0:T(1024)} %param.22) | copy-start | bytes 1990660
  316.3 259.7 %copy-start.45 = (f32[165888]{0:T(1024)S(1)}, f32[165888]{0:T(1024)}, u32[]{:S(2)}) copy-start(f32[165888]{0:T(1024)} %param.23) | copy-start | bytes 1990660
  576.1 10.6 %copy-start.41 = (f32[55368]{0:T(1024)S(1)}, f32[55368]{0:T(1024)}, u32[]{:S(2)}) copy-start(f32[55368]{0:T(1024)} %param.18) | copy-start | bytes 664420
  576.1 10.6 %copy-start.46 = (f32[55368]{0:T(1024)S(1)}, f32[55368]{0:T(1024)}, u32[]{:S(2)}) copy-start(f32[55368]{0:T(1024)} %param.19) | copy-start | bytes 664420
  576.1 10.6 %copy-start.47 = (f32[55368]{0:T(1024)S(1)}, f32[55368]{0:T(1024)}, u32[]{:S(2)}) copy-start(f32[55368]{0:T(1024)} %param.20) | copy-start | bytes 664420
  (48 other events, 126.7 us)
Sparse Core Ops, SparseCore 0:
  12.9 99.1 all-reduce.8
  114.8 56.0 all-gather.1
  229.8 11.7 reduce-scatter.2
  259.4 11.7 reduce-scatter.4
  311.7 248.3 all-reduce.12
  562.8 23.7 all-reduce.10
where the time goes:
time: 600 us; the launch traced here: 598 us
  waiting for transfers between devices  381 us (64%)
  local copies, waits for them, and re-layouts  88.9 us (15%)
  matrix products  58.9 us (10%)
  other arithmetic  27.6 us (5%)
  blocking collectives  23.4 us (4%)
  between operations  16.8 us (3%)
    unnamed x9, waiting for transfers between devices  348 us
    all_gather x1, waiting for transfers between devices, body(): lax.all_gather(low_params[1], 'shard', axis=0, tiled=True)  33.6 us
    concatenate x1, local copies, waits for them, and re-layouts, body(): jnp.concatenate([grad_w_query.reshape(-1), grad_w_key.reshape(-1), grad_w...  25.4 us
    slice x6, local copies, waits for them, and re-layouts, split_flattened(): pieces.append(flattened[offset:offset + width].reshape(shape))  18 us
    unnamed x105, local copies, waits for them, and re-layouts  13.8 us
    all_gather x1, blocking collectives, body(): lax.all_gather(ffn_half, 'ctx', axis=0, tiled=True)  12.8 us
  transfers between devices with their start and end apart: 6, of which 4 were waited for; matrix products, arithmetic and copies ran while one was open for 12% of the time, Pallas kernels for 0%

commit v1 on v0

--- a/solution.py
+++ b/solution.py
@@ -18,6 +18,21 @@
 decay_rate = 0.1
 adam_eps = 1e-08
 masked_score = -1e30
+
+
+def _play_terms(w_in):
+    current_arr = lax.axis_index("shard")
+    carry_out = lax.axis_size("shard")
+    mat_out, res, value_now = (carry_out, current_arr, w_in.shape[0])
+    w1 = jnp.zeros((*w_in.shape[:0], mat_out * value_now, *w_in.shape[1:]), w_in.dtype)
+    long_array = w_in
+    log = [(k0, (k0 + 1) % mat_out) for k0 in range(mat_out)]
+    for p in range(mat_out):
+        now = (res - p) % mat_out
+        w1 = lax.dynamic_update_slice_in_dim(w1, long_array, now * value_now, axis=0)
+        if p < mat_out - 1:
+            long_array = lax.ppermute(long_array, axis_name="shard", perm=log)
+    return w1
 
 
 def split_flattened(flattened, shapes):
@@ -188,7 +203,7 @@
     low_params = (attn_params.astype(jnp.bfloat16), ffn_params.astype(jnp.bfloat16))
     attn_whole, ffn_whole = (
         lax.all_gather(low_params[0], "shard", axis=0, tiled=True),
-        lax.all_gather(low_params[1], "shard", axis=0, tiled=True),
+        _play_terms(low_params[1]),
     )
     w_query, key_matrix, value_matrix, w_out, gain_one, gain_two = split_attention(attn_whole)
     w_gate, w_up, w_down = split_feedforward(ffn_whole)

time: 600 us -> 725 us (1.21); the launches traced: 598 us -> 714 us
  local copies, waits for them, and re-layouts: 88.9 us -> 186 us
  waiting for transfers between devices: 381 us -> 402 us
    ppermute x0 -> x15, waiting for transfers between devices: none -> 97.4 us  [_play_terms(): long_array = lax.ppermute(long_array, axis_name='shard', perm=log)]
    dynamic_update_slice x0 -> x15, local copies, waits for them, and re-layouts: none -> 92.5 us  [_play_terms(): lax.dynamic_update_slice_in_dim(w1, long_array, now * value_now, axis=0)]
    unnamed x9 -> x8, waiting for transfers between devices: 348 us -> 304 us
    all_gather x1 -> x0, waiting for transfers between devices: 33.6 us -> none  [body(): lax.all_gather(low_params[1], 'shard', axis=0, tiled=True)]
  transfers between devices with their start and end apart: 6 -> 20, of which waited for: 4 -> 14; matrix products, arithmetic and copies ran while one was open for 12% -> 22% of each run, Pallas kernels for 0% -> 0%
where the time goes in v1:
time: 725 us; the launch traced here: 714 us
  waiting for transfers between devices  402 us (55%)
  local copies, waits for them, and re-layouts  186 us (26%)
  matrix products  57.5 us (8%)
  other arithmetic  27.2 us (4%)
  blocking collectives  23.6 us (3%)
  between operations  17 us (2%)
    unnamed x8, waiting for transfers between devices  304 us
    ppermute x15, waiting for transfers between devices, _play_terms(): long_array = lax.ppermute(long_array, axis_name='shard', perm=log)  97.4 us
    dynamic_update_slice x15, local copies, waits for them, and re-layouts, _play_terms(): lax.dynamic_update_slice_in_dim(w1, long_array, now * value_now, axis=0)  92.5 us
    concatenate x1, local copies, waits for them, and re-layouts, body(): jnp.concatenate([grad_w_query.reshape(-1), grad_w_key.reshape(-1), grad_w...  26 us
    slice x6, local copies, waits for them, and re-layouts, split_flattened(): pieces.append(flattened[offset:offset + width].reshape(shape))  20.1 us
  transfers between devices with their start and end apart: 20, of which 14 were waited for; matrix products, arithmetic and copies ran while one was open for 22% of the time, Pallas kernels for 0%

profile of v1, /device:TPU:0, one launch (start us, length us, event | category | flops | bytes accessed | tf_op | source)
XLA Modules:
  0.0 714.2 jit_solution(2308748482732726075)
XLA Ops:
  11.3 9.8 %collective-permute-done = bf16[165888]{0:T(1024)(128)(2,1)S(1)} collective-permute-done((bf16[165888]{0:T(1024)(128)(2,1)S(1)}, bf16[165888]{0:T(1024)(128)(2,1)S(1)}, u32[]{:S(2)}, u32[]{:S(2)}) %collective-permute-start) | collective-permute-done | bytes 331808 | tf_op jit(solution)/shard_map/ppermute | solution.py:34
  21.0 9.2 %collective-permute-done.1 = bf16[165888]{0:T(1024)(128)(2,1)S(1)} collective-permute-done((bf16[165888]{0:T(1024)(128)(2,1)S(1)}, bf16[165888]{0:T(1024)(128)(2,1)S(1)}, u32[]{:S(2)}, u32[]{:S(2)}) %collective-permute-start.1) | collective-permute-done | bytes 331808 | tf_op jit(solution)/shard_map/ppermute | solution.py:34
  39.6 12.7 %collective-permute-done.3 = bf16[165888]{0:T(1024)(128)(2,1)S(1)} collective-permute-done((bf16[165888]{0:T(1024)(128)(2,1)S(1)}, bf16[165888]{0:T(1024)(128)(2,1)S(1)}, u32[]{:S(2)}, u32[]{:S(2)}) %collective-permute-start.3) | collective-permute-done | bytes 331808 | tf_op jit(solution)/shard_map/ppermute | solution.py:34
  52.6 12.5 %collective-permute-done.4 = bf16[165888]{0:T(1024)(128)(2,1)S(1)} collective-permute-done((bf16[165888]{0:T(1024)(128)(2,1)S(1)}, bf16[165888]{0:T(1024)(128)(2,1)S(1)}, u32[]{:S(2)}, u32[]{:S(2)}) %collective-permute-start.4) | collective-permute-done | bytes 331808 | tf_op jit(solution)/shard_map/ppermute | solution.py:34
  65.1 9.2 %collective-permute-done.5 = bf16[165888]{0:T(1024)(128)(2,1)S(1)} collective-permute-done((bf16[165888]{0:T(1024)(128)(2,1)S(1)}, bf16[165888]{0:T(1024)(128)(2,1)S(1)}, u32[]{:S(2)}, u32[]{:S(2)}) %collective-permute-start.5) | collective-permute-done | bytes 331808 | tf_op jit(solution)/shard_map/ppermute | solution.py:34
  86.7 49.7 %all-reduce.9.cloned.1.call-done = bf16[885888]{0:T(1024)(128)(2,1)} async-done(((bf16[885888]{0:T(1024)(128)(2,1)}), bf16[885888]{0:T(1024)(128)(2,1)}) %all-reduce.9.cloned.1.call-update) | async-done | bytes 1771792
  139.0 8.2 %collective-permute-done.8 = bf16[165888]{0:T(1024)(128)(2,1)} collective-permute-done((bf16[165888]{0:T(1024)(128)(2,1)S(1)}, bf16[165888]{0:T(1024)(128)(2,1)}, u32[]{:S(2)}, u32[]{:S(2)}) %collective-permute-start.8) | collective-permute-done | bytes 331808 | tf_op jit(solution)/shard_map/ppermute | solution.py:34
  149.0 7.7 %collective-permute-done.9 = bf16[165888]{0:T(1024)(128)(2,1)} collective-permute-done((bf16[165888]{0:T(1024)(128)(2,1)}, bf16[165888]{0:T(1024)(128)(2,1)}, u32[]{:S(2)}, u32[]{:S(2)}) %collective-permute-start.9) | collective-permute-done | bytes 331808 | tf_op jit(solution)/shard_map/ppermute | solution.py:34
  159.2 7.1 collective-permute-done.10
  166.4 9.4 %collective-permute-done.11 = bf16[165888]{0:T(1024)(128)(2,1)S(1)} collective-permute-done((bf16[165888]{0:T(1024)(128)(2,1)}, bf16[165888]{0:T(1024)(128)(2,1)S(1)}, u32[]{:S(2)}, u32[]{:S(2)}) %collective-permute-start.11) | collective-permute-done | bytes 331808 | tf_op jit(solution)/shard_map/ppermute | solution.py:34
  177.7 7.4 %collective-permute-done.12 = bf16[165888]{0:T(1024)(128)(2,1)} collective-permute-done((bf16[165888]{0:T(1024)(128)(2,1)S(1)}, bf16[165888]{0:T(1024)(128)(2,1)}, u32[]{:S(2)}, u32[]{:S(2)}) %collective-permute-start.12) | collective-permute-done | bytes 331808 | tf_op jit(solution)/shard_map/ppermute | solution.py:34
  203.2 6.2 dynamic_update_slice.62
  227.8 6.3 dynamic_update_slice.66
  240.2 6.2 dynamic_update_slice.68
  246.5 6.2 dynamic_update_slice.69
  252.7 6.2 dynamic_update_slice.70
  271.2 6.2 dynamic_update_slice.73
  312.4 30.6 %conditional.3 = (f32[256,9,64]{0,2,1:T(8,128)}, f32[512,3,64]{0,2,1:T(8,128)}, f32[512,3,64]{0,2,1:T(8,128)}) conditional(s32[]{:T(128)} %convert_element_type.112, () %tuple.30, (bf16[256,9,64]{0,2,1:T(8,128)(2,1)}, bf16[512,3,64]{0,2,1:T(8,128)(2,1)}, bf16[512,3,64]{0,2,1:T(8,128)(2,1)}, bf16[256,576]{0,1:T(8,128)(2,1)S(1)}, ...), branch_computations={%region_7.8_spmd, %region_8.11_spmd} | conditional | flops 254999808 | bytes 14379385 | solution.py:281
  312.4 30.6 %while.13 = (s32[]{:T(128)}, f32[3,256,3,64]{1,3,2,0:T(8,128)}, f32[3,512,64]{1,2,0:T(8,128)}, f32[3,512,64]{1,2,0:T(8,128)}, bf16[3,512,64]{1,2,0:T(8,128)(2,1)...) while((s32[]{:T(128)}, f32[3,256,3,64]{1,3,2,0:T(8,128)}, ...), condition=%wide.region_10.10_spmd, body=%wide.region_9.9_spmd.sunk | while | flops 254999808 | bytes 14379257 | solution.py:162
  372.7 11.2 %pad_maximum_fusion = f32[2654208]{0:T(1024)} fusion(f32[884736]{0:T(1024)} %reshape.299, f32[884736]{0:T(1024)} %reshape.298, f32[884736]{0:T(1024)} %reshape.297), kind=kLoop, calls=%fused_computation.50 | loop fusion | flops 5308416 | bytes 21233664 | tf_op jit(solution)/shard_map/concatenate | solution.py:267
  399.5 26.0 %concatenate.37 = f32[885888]{0:T(1024)} concatenate(f32[331776]{0:T(1024)S(1)} %copy-done.16, f32[110592]{0:T(1024)} %reshape.294, f32[110592]{0:T(1024)} %reshape.295, f32[331776]{0:T(1024)S(1)} %reshape.296, f32[576]{0:T(1024)} %get-tuple-element.157, f32[576]{0:T(1024)S(1)} %get-tuple-element.155), dimensions={0} | concatenate | bytes 7087104 | tf_op jit(solution)/shard_map/concatenate | solution.py:331
  431.3 245.5 %all-reduce.13.cloned.1.call-done = (f32[885888]{0:T(1024)}, f32[2654208]{0:T(1024)}) async-done(((f32[885888]{0:T(1024)}, f32[2654208]{0:T(1024)}), (f32[885888]{0:T(1024)}, f32[2654208]{0:T(1024)})) %all-reduce.13.cloned.1.call-update) | async-done | bytes 14160400
  679.9 12.8 %all_gather.19 = f32[165888]{0:T(1024)S(1)} all-gather(f32[82944]{0:T(1024)S(1)} %dynamic-slice.3), channel_id=1, replica_groups=mesh['shard'=16,'ctx'=2] {'ctx'}, dimensions={0}, use_global_device_ids=true | all-gather | bytes 995328 | tf_op jit(solution)/shard_map/all_gather | solution.py:348
  694.4 8.9 %all-reduce.11.cloned.1.call-done = f32[55368]{0:T(1024)} async-done(((f32[55368]{0:T(1024)}), f32[55368]{0:T(1024)}) %all-reduce.11.cloned.1.call-update) | async-done | bytes 221488
  (317 shorter events, 218.2 us)
Async XLA Ops:
  7.2 129.2 %all-reduce.9.cloned.1.call-start = ((), (), s32[]{:S(2)}) async-start(), calls=%async_computation.4 | async-start | bytes 3547136
  10.8 10.2 %collective-permute-start = (bf16[165888]{0:T(1024)(128)(2,1)S(1)}, bf16[165888]{0:T(1024)(128)(2,1)S(1)}, u32[]{:S(2)}, u32[]{:S(2)}) collective-permute-start(bf16[165888]{0:T(1024)(128)(2,1)S(1)} %get-tuple-element.190), channel_id=1, source_target_pairs={{0,2},{2,4},{4,6},{6,8},{8,10},{10,12},{12,14},{14,16},{16,18},{18... | collective-permute-start | bytes 995336 | tf_op jit(solution)/shard_map/ppermute | solution.py:34
  21.0 9.2 %collective-permute-start.1 = (bf16[165888]{0:T(1024)(128)(2,1)S(1)}, bf16[165888]{0:T(1024)(128)(2,1)S(1)}, u32[]{:S(2)}, u32[]{:S(2)}) collective-permute-start(bf16[165888]{0:T(1024)(128)(2,1)S(1)} %collective-permute-done), channel_id=1, source_target_pairs={{0,2},{2,4},{4,6},{6,8},{8,10},{10,12},{12,14},{14,16},{16,18},{18... | collective-permute-start | bytes 995336 | tf_op jit(solution)/shard_map/ppermute | solution.py:34
  30.3 9.2 %collective-permute-start.2 = (bf16[165888]{0:T(1024)(128)(2,1)S(1)}, bf16[165888]{0:T(1024)(128)(2,1)S(1)}, u32[]{:S(2)}, u32[]{:S(2)}) collective-permute-start(bf16[165888]{0:T(1024)(128)(2,1)S(1)} %collective-permute-done.1), channel_id=1, source_target_pairs={{0,2},{2,4},{4,6},{6,8},{8,10},{10,12},{12,14},{14,16},{16,18},{18... | collective-permute-start | bytes 995336 | tf_op jit(solution)/shard_map/ppermute | solution.py:34
  34.2 349.7 %reduce-scatter.3.cloned.1.call-start = ((), (), s32[]{:S(2)}) async-start(), calls=%async_computation.2 | async-start | bytes 589824 | tf_op jit(solution)/shard_map/reduce_scatter | solution.py:293
  39.5 12.8 %collective-permute-start.3 = (bf16[165888]{0:T(1024)(128)(2,1)S(1)}, bf16[165888]{0:T(1024)(128)(2,1)S(1)}, u32[]{:S(2)}, u32[]{:S(2)}) collective-permute-start(bf16[165888]{0:T(1024)(128)(2,1)S(1)} %collective-permute-done.2), channel_id=1, source_target_pairs={{0,2},{2,4},{4,6},{6,8},{8,10},{10,12},{12,14},{14,16},{16,18},{18... | collective-permute-start | bytes 995336 | tf_op jit(solution)/shard_map/ppermute | solution.py:34
  52.3 12.8 %collective-permute-start.4 = (bf16[165888]{0:T(1024)(128)(2,1)S(1)}, bf16[165888]{0:T(1024)(128)(2,1)S(1)}, u32[]{:S(2)}, u32[]{:S(2)}) collective-permute-start(bf16[165888]{0:T(1024)(128)(2,1)S(1)} %collective-permute-done.3), channel_id=1, source_target_pairs={{0,2},{2,4},{4,6},{6,8},{8,10},{10,12},{12,14},{14,16},{16,18},{18... | collective-permute-start | bytes 995336 | tf_op jit(solution)/shard_map/ppermute | solution.py:34
  52.5 294.9 %copy-start.33 = (f32[256,64]{0,1:T(8,128)}, f32[256,64]{0,1:T(8,128)S(1)}, u32[]{:S(2)}) copy-start(f32[256,64]{0,1:T(8,128)S(1)} %get-tuple-element.213) | copy-start | bytes 196612
  65.1 9.2 %collective-permute-start.5 = (bf16[165888]{0:T(1024)(128)(2,1)S(1)}, bf16[165888]{0:T(1024)(128)(2,1)S(1)}, u32[]{:S(2)}, u32[]{:S(2)}) collective-permute-start(bf16[165888]{0:T(1024)(128)(2,1)S(1)} %collective-permute-done.4), channel_id=1, source_target_pairs={{0,2},{2,4},{4,6},{6,8},{8,10},{10,12},{12,14},{14,16},{16,18},{18... | collective-permute-start | bytes 995336 | tf_op jit(solution)/shard_map/ppermute | solution.py:34
  74.3 12.4 %collective-permute-start.6 = (bf16[165888]{0:T(1024)(128)(2,1)S(1)}, bf16[165888]{0:T(1024)(128)(2,1)}, u32[]{:S(2)}, u32[]{:S(2)}) collective-permute-start(bf16[165888]{0:T(1024)(128)(2,1)S(1)} %collective-permute-done.5), channel_id=1, source_target_pairs={{0,2},{2,4},{4,6},{6,8},{8,10},{10,12},{12,14},{14,16},{16,18},{18... | collective-permute-start | bytes 995336 | tf_op jit(solution)/shard_map/ppermute | solution.py:34
  86.7 51.1 %collective-permute-start.7 = (bf16[165888]{0:T(1024)(128)(2,1)}, bf16[165888]{0:T(1024)(128)(2,1)S(1)}, u32[]{:S(2)}, u32[]{:S(2)}) collective-permute-start(bf16[165888]{0:T(1024)(128)(2,1)} %collective-permute-done.6), channel_id=1, source_target_pairs={{0,2},{2,4},{4,6},{6,8},{8,10},{10,12},{12,14},{14,16},{16,18},{18... | collective-permute-start | bytes 995336 | tf_op jit(solution)/shard_map/ppermute | solution.py:34
  137.8 9.4 %collective-permute-start.8 = (bf16[165888]{0:T(1024)(128)(2,1)S(1)}, bf16[165888]{0:T(1024)(128)(2,1)}, u32[]{:S(2)}, u32[]{:S(2)}) collective-permute-start(bf16[165888]{0:T(1024)(128)(2,1)S(1)} %collective-permute-done.7), channel_id=1, source_target_pairs={{0,2},{2,4},{4,6},{6,8},{8,10},{10,12},{12,14},{14,16},{16,18},{18... | collective-permute-start | bytes 995336 | tf_op jit(solution)/shard_map/ppermute | solution.py:34
  147.2 9.6 %collective-permute-start.9 = (bf16[165888]{0:T(1024)(128)(2,1)}, bf16[165888]{0:T(1024)(128)(2,1)}, u32[]{:S(2)}, u32[]{:S(2)}) collective-permute-start(bf16[165888]{0:T(1024)(128)(2,1)} %collective-permute-done.8), channel_id=1, source_target_pairs={{0,2},{2,4},{4,6},{6,8},{8,10},{10,12},{12,14},{14,16},{16,18},{18... | collective-permute-start | bytes 995336 | tf_op jit(solution)/shard_map/ppermute | solution.py:34
  156.7 9.6 %collective-permute-start.10 = (bf16[165888]{0:T(1024)(128)(2,1)}, bf16[165888]{0:T(1024)(128)(2,1)}, u32[]{:S(2)}, u32[]{:S(2)}) collective-permute-start(bf16[165888]{0:T(1024)(128)(2,1)} %collective-permute-done.9), channel_id=1, source_target_pairs={{0,2},{2,4},{4,6},{6,8},{8,10},{10,12},{12,14},{14,16},{16,18},{18... | collective-permute-start | bytes 995336 | tf_op jit(solution)/shard_map/ppermute | solution.py:34
  166.3 9.5 %collective-permute-start.11 = (bf16[165888]{0:T(1024)(128)(2,1)}, bf16[165888]{0:T(1024)(128)(2,1)S(1)}, u32[]{:S(2)}, u32[]{:S(2)}) collective-permute-start(bf16[165888]{0:T(1024)(128)(2,1)} %collective-permute-done.10), channel_id=1, source_target_pairs={{0,2},{2,4},{4,6},{6,8},{8,10},{10,12},{12,14},{14,16},{16,18},{18... | collective-permute-start | bytes 995336 | tf_op jit(solution)/shard_map/ppermute | solution.py:34
  175.7 9.3 %collective-permute-start.12 = (bf16[165888]{0:T(1024)(128)(2,1)S(1)}, bf16[165888]{0:T(1024)(128)(2,1)}, u32[]{:S(2)}, u32[]{:S(2)}) collective-permute-start(bf16[165888]{0:T(1024)(128)(2,1)S(1)} %collective-permute-done.11), channel_id=1, source_target_pairs={{0,2},{2,4},{4,6},{6,8},{8,10},{10,12},{12,14},{14,16},{16,18},{18... | collective-permute-start | bytes 995336 | tf_op jit(solution)/shard_map/ppermute | solution.py:34
  185.1 17.7 %collective-permute-start.13 = (bf16[165888]{0:T(1024)(128)(2,1)}, bf16[165888]{0:T(1024)(128)(2,1)}, u32[]{:S(2)}, u32[]{:S(2)}) collective-permute-start(bf16[165888]{0:T(1024)(128)(2,1)} %collective-permute-done.12), channel_id=1, source_target_pairs={{0,2},{2,4},{4,6},{6,8},{8,10},{10,12},{12,14},{14,16},{16,18},{18... | collective-permute-start | bytes 995336 | tf_op jit(solution)/shard_map/ppermute | solution.py:34
  202.8 74.7 %collective-permute-start.14 = (bf16[165888]{0:T(1024)(128)(2,1)}, bf16[165888]{0:T(1024)(128)(2,1)S(1)}, u32[]{:S(2)}, u32[]{:S(2)}) collective-permute-start(bf16[165888]{0:T(1024)(128)(2,1)} %collective-permute-done.13), channel_id=1, source_target_pairs={{0,2},{2,4},{4,6},{6,8},{8,10},{10,12},{12,14},{14,16},{16,18},{18... | collective-permute-start | bytes 995336 | tf_op jit(solution)/shard_map/ppermute | solution.py:34
  343.1 49.2 %reduce-scatter.5.cloned.1.call-start = ((), (), s32[]{:S(2)}) async-start(), calls=%async_computation.3 | async-start | bytes 589824 | tf_op jit(solution)/shard_map/reduce_scatter | solution.py:299
  372.7 304.0 %all-reduce.13.cloned.1.call-start = ((), (), s32[]{:S(2)}) async-start(), calls=%async_computation.6 | async-start | bytes 28327936
  425.6 277.7 %all-reduce.11.cloned.1.call-start = ((), (), s32[]{:S(2)}) async-start(), calls=%async_computation.5 | async-start | bytes 450560
  430.3 262.4 %copy-start.27 = (f32[165888]{0:T(1024)S(1)}, f32[165888]{0:T(1024)}, u32[]{:S(2)}) copy-start(f32[165888]{0:T(1024)} %param.21) | copy-start | bytes 1990660
  430.3 262.4 %copy-start.44 = (f32[165888]{0:T(1024)S(1)}, f32[165888]{0:T(1024)}, u32[]{:S(2)}) copy-start(f32[165888]{0:T(1024)} %param.22) | copy-start | bytes 1990660
  430.3 262.4 %copy-start.45 = (f32[165888]{0:T(1024)S(1)}, f32[165888]{0:T(1024)}, u32[]{:S(2)}) copy-start(f32[165888]{0:T(1024)} %param.23) | copy-start | bytes 1990660
  (70 other events, 979.4 us)
Sparse Core Ops, SparseCore 0:
  34.3 102.0 all-reduce.8
  343.2 14.3 reduce-scatter.2
  372.8 14.3 reduce-scatter.4
  425.7 250.9 all-reduce.12
  679.4 23.7 all-reduce.10
